TPU v7x, 32 devices: a whole 2x2x4 slice. The times are simulated.
32 devices in a mesh: dp: 4 (over y, x), seq: 8 (over z, core).
Axes of the slice: x: 2, y: 2, z: 4, core: 2. Of those that a mesh axis runs over, the one named last changes fastest.
Arguments:
- tiles: bfloat16 [4, 8192, 768], P('dp', 'seq'), may hold values from -48 to 48
- tile_count: int32 [4], P('dp'), may hold values from 4097 to 8192
- offsets: int32 [16], replicated, may hold values from 0 to 15
- w_query: bfloat16 [768, 768], replicated, may hold values from -0.375 to 0.375
- w_key: bfloat16 [768, 768], replicated, may hold values from -0.375 to 0.375
- w_value: bfloat16 [768, 768], replicated, may hold values from -0.21875 to 0.21875
- w_out: bfloat16 [768, 768], replicated, may hold values from -0.21875 to 0.21875
- cotangent: bfloat16 [4, 8192, 768], P('dp', 'seq'), may hold values from -0.046875 to 0.046875
Outputs:
- branch: bfloat16 [4, 8192, 768], P('dp', 'seq')
- grad_out: float32 [768, 768], P(None, 'seq')
All inputs are finite; a program needn't handle non-finite values.
Results may differ from a plain program's by a relative error of at most 0.0095.
The roundings to bfloat16 on the way count: a program that leaves them out, or rounds other values in their place, can miss the bound.
Values may be sent and summed in bfloat16 or wider, within the bound.
A program may use at most 128 MiB of HBM per device.

v0:
```python
import jax
import jax.numpy as jnp
from jax import lax
from jax.sharding import PartitionSpec as P

D = 768
ATTENTION_HEADS = 16
HEAD_SIZE = 48
SEG = 1024
RATE = 16
NEGATIVE_FLOOR = -1e30
head_group = 4


def project(inputs, weight):
    return jnp.dot(inputs, weight, preferred_element_type=jnp.float32).astype(jnp.bfloat16)


def select_rows(tensor, offsets):
    segment_height = tensor.shape[0]
    grouped = tensor.reshape(segment_height // RATE, RATE, ATTENTION_HEADS, HEAD_SIZE)
    onehot = (jnp.arange(RATE, dtype=jnp.int32)[:, None] == offsets[None, :]).astype(jnp.bfloat16)
    return jnp.einsum("arhd,rh->ahd", grouped, onehot, preferred_element_type=jnp.float32).astype(
        jnp.bfloat16
    )


def local_attention(query_proj, key_proj, value_proj, is_live):
    segment_height = query_proj.shape[0]
    segments = segment_height // SEG
    groups = ATTENTION_HEADS // head_group
    query_seg = query_proj.reshape(segments, SEG, groups, head_group, HEAD_SIZE)
    key_seg = key_proj.reshape(segments, SEG, groups, head_group, HEAD_SIZE)
    value_seg = value_proj.reshape(segments, SEG, groups, head_group, HEAD_SIZE)
    alive_seg = is_live.reshape(segments, SEG)

    def one_group(index):
        query_part = lax.dynamic_index_in_dim(query_seg, index, 2, keepdims=False)
        key_part = lax.dynamic_index_in_dim(key_seg, index, 2, keepdims=False)
        value_part = lax.dynamic_index_in_dim(value_seg, index, 2, keepdims=False)
        scores = jnp.einsum(
            "sqhd,skhd->shqk", query_part, key_part, preferred_element_type=jnp.float32
        ) * HEAD_SIZE ** (-0.5)
        scores = jnp.where(alive_seg[:, None, None, :], scores, NEGATIVE_FLOOR)
        maxima = jnp.max(scores, axis=-1)
        weights = jnp.exp(scores - maxima[..., None])
        totals = jnp.sum(weights, axis=-1)
        weighted = jnp.einsum(
            "shqk,skhd->sqhd",
            weights.astype(jnp.bfloat16),
            value_part,
            preferred_element_type=jnp.float32,
        )
        return (maxima, totals, weighted)

    maxima, totals, weighted = lax.map(one_group, jnp.arange(groups, dtype=jnp.int32))
    maxima = maxima.transpose(1, 3, 0, 2).reshape(segment_height, ATTENTION_HEADS)
    totals = totals.transpose(1, 3, 0, 2).reshape(segment_height, ATTENTION_HEADS)
    weighted = weighted.transpose(1, 2, 0, 3, 4).reshape(segment_height, ATTENTION_HEADS, HEAD_SIZE)
    return (maxima, totals, weighted)


def combine(local, dilated_branch, offsets, is_live):
    local_max, local_total, local_sum = local
    dilated_row_max, dilated_value_total, dilated_row_sum = dilated_branch
    segment_height = local_max.shape[0]
    dilation_match = jnp.arange(RATE, dtype=jnp.int32)[:, None] == offsets[None, :]
    dense_row_max = jnp.where(
        dilation_match[None], dilated_row_max[:, None, :], NEGATIVE_FLOOR
    ).reshape(segment_height, ATTENTION_HEADS)
    dense_value_total = jnp.where(
        dilation_match[None], dilated_value_total[:, None, :], 0.0
    ).reshape(segment_height, ATTENTION_HEADS)
    dense_row_sum = jnp.where(
        dilation_match[None, :, :, None], dilated_row_sum[:, None], 0.0
    ).reshape(segment_height, ATTENTION_HEADS, HEAD_SIZE)
    top = jnp.maximum(local_max, dense_row_max)
    near = jnp.exp(local_max - top)
    far = jnp.exp(dense_row_max - top)
    attn = (near[..., None] * local_sum + far[..., None] * dense_row_sum) / (
        near * local_total + far * dense_value_total
    )[..., None]
    attn = jnp.where(is_live[:, None, None], attn, 0.0)
    return attn.reshape(segment_height, D).astype(jnp.bfloat16)


def body(tiles, tile_count, offsets, w_query, w_key, w_value, w_out, cotangent):
    inputs = tiles[0]
    segment_height = inputs.shape[0]
    shard_rank = lax.axis_index("seq")
    live_count = tile_count[0]
    query_proj = project(inputs, w_query).reshape(segment_height, ATTENTION_HEADS, HEAD_SIZE)
    key_proj = project(inputs, w_key).reshape(segment_height, ATTENTION_HEADS, HEAD_SIZE)
    value_proj = project(inputs, w_value).reshape(segment_height, ATTENTION_HEADS, HEAD_SIZE)
    positions = shard_rank * segment_height + jnp.arange(segment_height, dtype=jnp.int32)
    is_live = positions < live_count
    local = local_attention(query_proj, key_proj, value_proj, is_live)
    picked = segment_height // RATE
    query_sel = select_rows(query_proj, offsets)
    key_sel = select_rows(key_proj, offsets)
    value_sel = select_rows(value_proj, offsets)
    score_scale = HEAD_SIZE ** (-0.5)
    portion = (
        lax.all_gather(key_sel.reshape(picked, D), "seq", axis=0, tiled=True),
        lax.all_gather(value_sel.reshape(picked, D), "seq", axis=0, tiled=True),
    )
    old_max = jnp.full((picked, ATTENTION_HEADS), NEGATIVE_FLOOR, jnp.float32)
    key_part = portion[0].reshape(portion[0].shape[0], ATTENTION_HEADS, HEAD_SIZE)
    value_part = portion[1].reshape(portion[1].shape[0], ATTENTION_HEADS, HEAD_SIZE)
    amount = key_part.shape[0]
    key_live = jnp.arange(amount, dtype=jnp.int32)[:, None] * RATE + offsets[None, :] < live_count
    scores = (
        jnp.einsum("qhd,khd->qhk", query_sel, key_part, preferred_element_type=jnp.float32)
        * score_scale
    )
    scores = jnp.where(key_live.T[None], scores, NEGATIVE_FLOOR)
    new_max = jnp.maximum(old_max, jnp.max(scores, axis=-1))
    weights = jnp.exp(scores - new_max[..., None])
    new_total = jnp.sum(weights, axis=-1)
    new_sum = jnp.einsum(
        "qhk,khd->qhd", weights.astype(jnp.bfloat16), value_part, preferred_element_type=jnp.float32
    )
    dilated_branch = (new_max, new_total, new_sum)
    attn = combine(local, dilated_branch, offsets, is_live)
    branch = jnp.dot(attn, w_out, preferred_element_type=jnp.float32).astype(jnp.bfloat16)[None]
    gradient_in = cotangent[0]
    shares = lax.psum_scatter(
        jnp.einsum("tc,td->cd", gradient_in, attn, preferred_element_type=jnp.float32),
        "seq",
        scatter_dimension=0,
        tiled=True,
    )
    grad_part = lax.psum(shares.astype(jnp.bfloat16), "dp").astype(jnp.float32).T
    return (branch, grad_part)


def solution(mesh):
    in_specs = (P("dp", "seq", None), P("dp"), P(), P(), P(), P(), P(), P("dp", "seq", None))
    out_specs = (P("dp", "seq", None), P(None, "seq"))
    return jax.shard_map(body, mesh=mesh, in_specs=in_specs, out_specs=out_specs, check_vma=False)
```

profile of v0, /device:TPU:0, one launch (start us, length us, event | category | flops | bytes accessed | tf_op | source)
XLA Modules:
  0.0 290.6 jit_solution(8163011718679875207)
XLA Ops:
  9.7 2.8 convolution_convert_fusion.3
  12.5 2.6 convolution_convert_fusion.2
  15.1 2.6 convolution_convert_fusion.1
  17.7 2.8 copy.49
  20.4 1.6 copy.45
  22.1 1.6 copy.47
  23.6 7.2 %reshape_reshape.22 = bf16[64,16,16,48]{3,2,1,0:T(8,128)(2,1)} reshape(bf16[1024,768]{1,0:T(8,128)(2,1)} %copy.47) | data formatting | bytes 3145728 | tf_op jit(solution)/shard_map/reshape;reshape | solution.py:21
  30.8 7.2 %reshape_reshape.21 = bf16[64,16,16,48]{3,2,1,0:T(8,128)(2,1)} reshape(bf16[1024,768]{1,0:T(8,128)(2,1)} %copy.45) | data formatting | bytes 3145728 | tf_op jit(solution)/shard_map/reshape;reshape | solution.py:21
  38.0 7.2 %reshape_reshape.23 = bf16[64,16,16,48]{3,2,1,0:T(8,128)(2,1)} reshape(bf16[1024,768]{1,0:T(8,128)(2,1)} %copy.49) | data formatting | bytes 3145728 | tf_op jit(solution)/shard_map/reshape;reshape | solution.py:21
  45.2 9.0 %multiply_reduce_fusion.1 = (bf16[16,64,48]{2,0,1:T(8,128)(2,1)S(1)}, bf16[16,64,48]{2,0,1:T(8,128)(2,1)}, bf16[16,64,48]{2,0,1:T(8,128)(2,1)}) fusion(f32[16,16]{0,1:T(8,128)S(1)} %copy.80, bf16[64,16,16,48]{3,2,1,0:T(8,128)(2,1)} %reshape_reshape.22, bf16[64,16,16,48]{3,2,1,0:T(8,128)(2,1)} %reshape_reshape.23, bf16[64,16,16,48]{3,2,1,0:T(8,128)(2,1)} %reshape_reshape.21), kind=kLoop, calls=%fused_computation.25 | loop fusion | flops 6930432 | bytes 5014528
  55.1 1.2 reshape.266
  56.3 1.2 reshape.263
  57.5 18.4 %all_gather.6 = bf16[512,768]{1,0:T(8,128)(2,1)} all-gather(bf16[64,768]{1,0:T(8,128)(2,1)S(1)} %reshape.263), channel_id=1, replica_groups=mesh['dp'=4,'seq'=8] {'seq'}, dimensions={0}, use_global_device_ids=true | all-gather | bytes 884736 | tf_op jit(solution)/shard_map/all_gather | solution.py:104
  76.0 2.3 copy.46
  78.3 16.6 %all_gather.7 = bf16[512,768]{1,0:T(8,128)(2,1)} all-gather(bf16[64,768]{1,0:T(8,128)(2,1)S(1)} %reshape.266), channel_id=1, replica_groups=mesh['dp'=4,'seq'=8] {'seq'}, dimensions={0}, use_global_device_ids=true | all-gather | bytes 884736 | tf_op jit(solution)/shard_map/all_gather | solution.py:105
  94.9 2.3 copy.50
  97.3 1.8 bitcast_reduce_fusion
  99.1 1.4 fusion.34
  102.1 1.7 broadcast_in_dim.151
  103.8 1.3 broadcast_in_dim.152
  105.1 1.7 broadcast_in_dim.159
  106.8 1.3 broadcast_in_dim.160
  108.7 66.5 %while.15 = (s32[]{:T(128)}, f32[4,1,4,1024]{3,2,1,0:T(4,128)}, f32[4,1,4,1024]{3,2,1,0:T(4,128)}, f32[4,1,1024,4,48]{2,4,3,1,0:T(8,128)}, s32[4]{0:T(128)S(1)},...) while((s32[]{:T(128)}, f32[4,1,4,1024]{3,2,1,0:T(4,128)}, ...), condition=%wide.region_3.4_spmd.clone, body=%wide.region_0.3_spmd.clone.sunk | while | flops 851437568 | bytes 52434116 | solution.py:56
  111.6 3.3 %fusion.70 = (f32[4,1024]{1,0:T(4,128)S(1)}, f32[4,1024,1024]{1,2,0:T(8,128)S(1)}) fusion(pred[1024]{0:T(1024)(128)(4,1)S(1)} %add_compare_fusion.4, bf16[1,1024,4,4,48]{1,4,3,2,0:T(8,128)(2,1)S(1)} %get-tuple-element.223, s32[]{:T(128)S(6)} %select_n.128, bf16[1,1024,4,4,48]{1,4,3,2,0:T(8,128)(2,1)S(1)} %get-tuple-element.222), kind=kOutput, calls=%fused_computation.3.clone.1 | convolution fusion | flops 415232000 | bytes 17582080 | tf_op jit(solution)/shard_map/while/body/eval_jaxpr/sqhd,skhd->shqk/dot_general | solution.py:41
  115.0 4.1 %fusion.71 = f32[4,1024]{1,0:T(4,128)S(1)} fusion(f32[4,1024,1024]{1,2,0:T(8,128)S(1)} %get-tuple-element.187, f32[4,1024]{1,0:T(4,128)S(1)} %get-tuple-element.188, pred[1024]{0:T(1024)(128)(4,1)S(1)} %add_compare_fusion.4), kind=kLoop, calls=%fused_computation.5.clone.1 | loop fusion | flops 16773120 | bytes 16811008 | tf_op jit(solution)/shard_map/while/body/eval_jaxpr/reduce_sum | solution.py:47
  119.1 5.7 %fusion.72 = f32[4,1,1024,4,48]{2,4,3,1,0:T(8,128)} fusion(f32[4,1,1024,4,48]{2,4,3,1,0:T(8,128)} %get-tuple-element.207, s32[]{:T(128)S(6)} %copy.89, f32[4,1024,1024]{1,2,0:T(8,128)S(1)} %get-tuple-element.187, f32[4,1024]{1,0:T(4,128)S(1)} %get-tuple-element.188, pred[1024]{0:T(1024)(128)(4,1)S(1)} %add_compare_fusion.4, ...), kind=kOutput, calls=%fused_computation.9.clone.1 | convolution fusion | flops 419430400 | bytes 17974280 | tf_op jit(solution)/shard_map/while/body/eval_jaxpr/shqk,skhd->sqhd/dot_general | solution.py:48
  128.3 3.3 %fusion.70 = (f32[4,1024]{1,0:T(4,128)S(1)}, f32[4,1024,1024]{1,2,0:T(8,128)S(1)}) fusion(pred[1024]{0:T(1024)(128)(4,1)S(1)} %add_compare_fusion.4, bf16[1,1024,4,4,48]{1,4,3,2,0:T(8,128)(2,1)S(1)} %get-tuple-element.223, s32[]{:T(128)S(6)} %select_n.128, bf16[1,1024,4,4,48]{1,4,3,2,0:T(8,128)(2,1)S(1)} %get-tuple-element.222), kind=kOutput, calls=%fused_computation.3.clone.1 | convolution fusion | flops 415232000 | bytes 17582080 | tf_op jit(solution)/shard_map/while/body/eval_jaxpr/sqhd,skhd->shqk/dot_general | solution.py:41
  131.6 4.1 %fusion.71 = f32[4,1024]{1,0:T(4,128)S(1)} fusion(f32[4,1024,1024]{1,2,0:T(8,128)S(1)} %get-tuple-element.187, f32[4,1024]{1,0:T(4,128)S(1)} %get-tuple-element.188, pred[1024]{0:T(1024)(128)(4,1)S(1)} %add_compare_fusion.4), kind=kLoop, calls=%fused_computation.5.clone.1 | loop fusion | flops 16773120 | bytes 16811008 | tf_op jit(solution)/shard_map/while/body/eval_jaxpr/reduce_sum | solution.py:47
  135.8 5.6 %fusion.72 = f32[4,1,1024,4,48]{2,4,3,1,0:T(8,128)} fusion(f32[4,1,1024,4,48]{2,4,3,1,0:T(8,128)} %get-tuple-element.207, s32[]{:T(128)S(6)} %copy.89, f32[4,1024,1024]{1,2,0:T(8,128)S(1)} %get-tuple-element.187, f32[4,1024]{1,0:T(4,128)S(1)} %get-tuple-element.188, pred[1024]{0:T(1024)(128)(4,1)S(1)} %add_compare_fusion.4, ...), kind=kOutput, calls=%fused_computation.9.clone.1 | convolution fusion | flops 419430400 | bytes 17974280 | tf_op jit(solution)/shard_map/while/body/eval_jaxpr/shqk,skhd->sqhd/dot_general | solution.py:48
  144.9 3.3 %fusion.70 = (f32[4,1024]{1,0:T(4,128)S(1)}, f32[4,1024,1024]{1,2,0:T(8,128)S(1)}) fusion(pred[1024]{0:T(1024)(128)(4,1)S(1)} %add_compare_fusion.4, bf16[1,1024,4,4,48]{1,4,3,2,0:T(8,128)(2,1)S(1)} %get-tuple-element.223, s32[]{:T(128)S(6)} %select_n.128, bf16[1,1024,4,4,48]{1,4,3,2,0:T(8,128)(2,1)S(1)} %get-tuple-element.222), kind=kOutput, calls=%fused_computation.3.clone.1 | convolution fusion | flops 415232000 | bytes 17582080 | tf_op jit(solution)/shard_map/while/body/eval_jaxpr/sqhd,skhd->shqk/dot_general | solution.py:41
  148.3 4.1 %fusion.71 = f32[4,1024]{1,0:T(4,128)S(1)} fusion(f32[4,1024,1024]{1,2,0:T(8,128)S(1)} %get-tuple-element.187, f32[4,1024]{1,0:T(4,128)S(1)} %get-tuple-element.188, pred[1024]{0:T(1024)(128)(4,1)S(1)} %add_compare_fusion.4), kind=kLoop, calls=%fused_computation.5.clone.1 | loop fusion | flops 16773120 | bytes 16811008 | tf_op jit(solution)/shard_map/while/body/eval_jaxpr/reduce_sum | solution.py:47
  152.4 5.6 %fusion.72 = f32[4,1,1024,4,48]{2,4,3,1,0:T(8,128)} fusion(f32[4,1,1024,4,48]{2,4,3,1,0:T(8,128)} %get-tuple-element.207, s32[]{:T(128)S(6)} %copy.89, f32[4,1024,1024]{1,2,0:T(8,128)S(1)} %get-tuple-element.187, f32[4,1024]{1,0:T(4,128)S(1)} %get-tuple-element.188, pred[1024]{0:T(1024)(128)(4,1)S(1)} %add_compare_fusion.4, ...), kind=kOutput, calls=%fused_computation.9.clone.1 | convolution fusion | flops 419430400 | bytes 17974280 | tf_op jit(solution)/shard_map/while/body/eval_jaxpr/shqk,skhd->sqhd/dot_general | solution.py:48
  161.5 3.3 %fusion.70 = (f32[4,1024]{1,0:T(4,128)S(1)}, f32[4,1024,1024]{1,2,0:T(8,128)S(1)}) fusion(pred[1024]{0:T(1024)(128)(4,1)S(1)} %add_compare_fusion.4, bf16[1,1024,4,4,48]{1,4,3,2,0:T(8,128)(2,1)S(1)} %get-tuple-element.223, s32[]{:T(128)S(6)} %select_n.128, bf16[1,1024,4,4,48]{1,4,3,2,0:T(8,128)(2,1)S(1)} %get-tuple-element.222), kind=kOutput, calls=%fused_computation.3.clone.1 | convolution fusion | flops 415232000 | bytes 17582080 | tf_op jit(solution)/shard_map/while/body/eval_jaxpr/sqhd,skhd->shqk/dot_general | solution.py:41
  164.9 4.1 %fusion.71 = f32[4,1024]{1,0:T(4,128)S(1)} fusion(f32[4,1024,1024]{1,2,0:T(8,128)S(1)} %get-tuple-element.187, f32[4,1024]{1,0:T(4,128)S(1)} %get-tuple-element.188, pred[1024]{0:T(1024)(128)(4,1)S(1)} %add_compare_fusion.4), kind=kLoop, calls=%fused_computation.5.clone.1 | loop fusion | flops 16773120 | bytes 16811008 | tf_op jit(solution)/shard_map/while/body/eval_jaxpr/reduce_sum | solution.py:47
  169.0 5.6 %fusion.72 = f32[4,1,1024,4,48]{2,4,3,1,0:T(8,128)} fusion(f32[4,1,1024,4,48]{2,4,3,1,0:T(8,128)} %get-tuple-element.207, s32[]{:T(128)S(6)} %copy.89, f32[4,1024,1024]{1,2,0:T(8,128)S(1)} %get-tuple-element.187, f32[4,1024]{1,0:T(4,128)S(1)} %get-tuple-element.188, pred[1024]{0:T(1024)(128)(4,1)S(1)} %add_compare_fusion.4, ...), kind=kOutput, calls=%fused_computation.9.clone.1 | convolution fusion | flops 419430400 | bytes 17974280 | tf_op jit(solution)/shard_map/while/body/eval_jaxpr/shqk,skhd->sqhd/dot_general | solution.py:48
  176.9 4.9 %broadcast_in_dim.156 = f32[64,16,16,48]{3,2,1,0:T(8,128)} broadcast(f32[64,16,48]{2,1,0:T(8,128)} %copy.51), dimensions={0,2,3} | broadcast | bytes 3342336 | tf_op jit(solution)/shard_map/jit(_where)/broadcast_in_dim | solution.py:74
  181.9 6.6 %copy.53 = f32[1024,16,48]{0,2,1:T(8,128)} copy(f32[1024,16,48]{2,1,0:T(8,128)} %bitcast.162) | data formatting | bytes 6291456 | tf_op jit(solution)/shard_map/jit(_where)/broadcast_in_dim | solution.py:74
  188.5 4.0 %fusion.32 = bf16[1024,16,48]{0,2,1:T(8,128)(2,1)S(1)} fusion(f32[1024,16,48]{0,2,1:T(8,128)} %copy.53, f32[4,1,1024,4,48]{2,4,3,1,0:T(8,128)} %get-tuple-element.52, f32[1024,16]{0,1:T(8,128)S(1)} %get-tuple-element.111, f32[1024,16]{0,1:T(8,128)S(1)} %get-tuple-element.113, f32[1024,16]{0,1:T(8,128)S(1)} %get-tuple-element.112, ...), kind=kLoop, calls=%fused_computation.37 | loop fusion | flops 5505024 | bytes 8078336 | tf_op jit(solution)/shard_map/convert_element_type | solution.py:84
  192.5 2.9 convolution_bitcast_fusion
  195.4 3.0 %copy.78 = f32[768,768]{1,0:T(8,128)} copy(f32[768,768]{0,1:T(8,128)} %convolution_bitcast_fusion) | data formatting | bytes 4718592
  198.5 7.9 %broadcast_in_dim.157 = f32[1024,768]{1,0:T(8,128)} reshape(f32[64,16,16,48]{3,2,1,0:T(8,128)} %broadcast_in_dim.156) | data formatting | bytes 6291456 | tf_op jit(solution)/shard_map/jit(_where)/broadcast_in_dim | solution.py:74
  206.5 3.6 %copy.52 = f32[1024,768]{0,1:T(8,128)} copy(f32[1024,768]{1,0:T(8,128)} %broadcast_in_dim.157) | data formatting | bytes 6291456 | tf_op jit(solution)/shard_map/jit(_where)/broadcast_in_dim | solution.py:74
  210.0 3.9 %fusion.31 = bf16[1024,768]{0,1:T(8,128)(2,1)S(1)} fusion(f32[1024,768]{0,1:T(8,128)} %copy.52, f32[4,1,1024,4,48]{2,4,3,1,0:T(8,128)} %get-tuple-element.52, f32[1024,16]{0,1:T(8,128)S(1)} %get-tuple-element.111, f32[1024,16]{0,1:T(8,128)S(1)} %get-tuple-element.113, f32[1024,16]{0,1:T(8,128)S(1)} %get-tuple-element.112, ...), kind=kLoop, calls=%fused_computation.36 | loop fusion | flops 5505024 | bytes 8078336 | tf_op jit(solution)/shard_map/convert_element_type | solution.py:84
  213.9 23.1 %reduce-scatter.4.cloned.1.call-done = f32[96,768]{1,0:T(8,128)} async-done(((f32[768,768]{1,0:T(8,128)}), f32[96,768]{1,0:T(8,128)}) %reduce-scatter.4.cloned.1.call-update) | async-done | bytes 294928
  236.9 1.8 copy.79
  238.8 4.0 %fusion.40 = bf16[1,1024,768]{2,1,0:T(8,128)(2,1)} fusion(bf16[1024,768]{0,1:T(8,128)(2,1)S(1)} %fusion.31, bf16[768,768]{1,0:T(8,128)(2,1)} %param.16), kind=kOutput, calls=%fused_computation.53 | convolution fusion | flops 1208745984 | bytes 4325376 | tf_op jit(solution)/shard_map/dot_general | solution.py:125
  242.7 39.3 %all-reduce.2.cloned.1.call-done = bf16[768,96]{1,0:T(8,128)(2,1)} async-done(((bf16[768,96]{1,0:T(8,128)(2,1)}), bf16[768,96]{1,0:T(8,128)(2,1)}) %all-reduce.2.cloned.1.call-update) | async-done | bytes 147472 | tf_op jit(solution)/shard_map/psum | solution.py:133
  282.0 1.8 copy.54
  (60 shorter events, 14.3 us)
Async XLA Ops:
  7.2 2.5 copy-start
  7.2 229.8 %reduce-scatter.4.cloned.1.call-start = ((), (), s32[]{:S(2)}) async-start(), calls=%async_computation.2 | async-start | bytes 2654208
  9.6 2.8 copy-start.11
  12.5 2.6 copy-start.12
  17.7 2.8 copy-start.2
  57.5 39.7 %copy-start.3 = (bf16[16,64,48]{1,2,0:T(8,128)(2,1)S(1)}, bf16[16,64,48]{1,2,0:T(8,128)(2,1)}, u32[]{:S(2)}) copy-start(bf16[16,64,48]{1,2,0:T(8,128)(2,1)} %copy.70) | copy-start | bytes 294916
  76.0 21.2 %copy-start.8 = (s32[512]{0:T(512)S(1)}, s32[512]{0:T(512)}, u32[]{:S(2)}) copy-start(s32[512]{0:T(512)} %iota_multiply_fusion) | copy-start | bytes 6148
  76.0 21.2 %copy-start.9 = (s32[16]{0:T(128)S(1)}, s32[16]{0:T(128)}, u32[]{:S(2)}) copy-start(s32[16]{0:T(128)} %param.12) | copy-start | bytes 196
  97.2 3.2 %copy-start.4 = (bf16[512,768]{0,1:T(8,128)(2,1)S(1)}, bf16[512,768]{0,1:T(8,128)(2,1)}, u32[]{:S(2)}) copy-start(bf16[512,768]{0,1:T(8,128)(2,1)} %copy.50) | copy-start | bytes 2359300
  99.1 1.4 copy-start.5
  181.9 6.6 %copy-start.6 = (pred[1024]{0:T(1024)(128)(4,1)S(1)}, pred[1024]{0:T(1024)(128)(4,1)}, u32[]{:S(2)}) copy-start(pred[1024]{0:T(1024)(128)(4,1)} %add_compare_fusion.2) | copy-start | bytes 3076
  188.5 4.0 %copy-start.10 = (bf16[1,1024,768]{2,1,0:T(8,128)(2,1)S(1)}, bf16[1,1024,768]{2,1,0:T(8,128)(2,1)}, u32[]{:S(2)}) copy-start(bf16[1,1024,768]{2,1,0:T(8,128)(2,1)} %param.17) | copy-start | bytes 4718596
  198.5 83.5 %all-reduce.2.cloned.1.call-start = ((), (), s32[]{:S(2)}) async-start(), calls=%async_computation.1 | async-start | bytes 393216 | tf_op jit(solution)/shard_map/psum | solution.py:133
  206.5 3.6 %copy-start.7 = (pred[1024]{0:T(1024)(128)(4,1)S(1)}, pred[1024]{0:T(1024)(128)(4,1)}, u32[]{:S(2)}) copy-start(pred[1024]{0:T(1024)(128)(4,1)} %add_compare_fusion.2) | copy-start | bytes 3076
  238.7 45.0 %copy-start.1 = (bf16[1,1024,768]{2,1,0:T(8,128)(2,1)S(1)}, bf16[1,1024,768]{2,1,0:T(8,128)(2,1)}, u32[]{:S(2)}) copy-start(bf16[1,1024,768]{2,1,0:T(8,128)(2,1)} %param.10) | copy-start | bytes 4718596
Sparse Core Ops, SparseCore 0:
  198.6 38.3 reduce-scatter.3
  240.4 41.5 all-reduce.1
where the time goes:
time: 292 us; the launch traced here: 291 us
  local copies, waits for them, and re-layouts  79 us (27%)
  waiting for transfers between devices  62.4 us (21%)
  matrix products  53.2 us (18%)
  other arithmetic  39.2 us (13%)
  blocking collectives  35 us (12%)
  between operations  14.9 us (5%)
  loops' own time  6.89 us (2%)
    psum x1, waiting for transfers between devices, body(): lax.psum(shares.astype(jnp.bfloat16), 'dp').astype(jnp.float32)  39.3 us
    unnamed x3, waiting for transfers between devices  23.1 us
    broadcast_in_dim x4, local copies, waits for them, and re-layouts, combine(): jnp.where(dilation_match[None, :, :, None], dilated_row_sum[:, None], 0.0)  23 us
    dot_general x4, matrix products, one_group(): jnp.einsum('shqk,skhd->sqhd', weights.astype(jnp.bfloat16), value_part, p...  22.5 us
    another operation x3, local copies, waits for them, and re-layouts, select_rows(): tensor.reshape(segment_height // RATE, RATE, ATTENTION_HEADS, HEAD_SIZE)  21.5 us
    all_gather x1, blocking collectives, body(): lax.all_gather(key_sel.reshape(picked, D), 'seq', axis=0, tiled=True)  18.4 us
    all_gather x1, blocking collectives, body(): lax.all_gather(value_sel.reshape(picked, D), 'seq', axis=0, tiled=True)  16.6 us
    reduce_sum x4, other arithmetic, one_group(): totals = jnp.sum(weights, axis=-1)  16.4 us
  transfers between devices with their start and end apart: 2, of which 2 were waited for; matrix products, arithmetic and copies ran while one was open for 7% of the time, Pallas kernels for 0%

commit v1 on v0

--- a/solution.py
+++ b/solution.py
@@ -130,7 +130,10 @@
         scatter_dimension=0,
         tiled=True,
     )
-    grad_part = lax.psum(shares.astype(jnp.bfloat16), "dp").astype(jnp.float32).T
+    return_all_table_in = lambda field_in, lane_axis: lax.all_gather(field_in, lane_axis).sum(
+        axis=0
+    )
+    grad_part = return_all_table_in(shares.astype(jnp.bfloat16), "dp").astype(jnp.float32).T
     return (branch, grad_part)
 
 

time: 292 us -> 259 us (0.89)
  waiting for transfers between devices: 62.4 us -> 20.4 us
  blocking collectives: 35 us -> 46.1 us
  local copies, waits for them, and re-layouts: 79 us -> 75.7 us
    psum x1 -> x0, waiting for transfers between devices: 39.3 us -> none  [body(): lax.psum(shares.astype(jnp.bfloat16), 'dp').astype(jnp.float32)]
    unnamed x3 -> x1, waiting for transfers between devices: 23.1 us -> 0.02 us
    reduce_scatter x0 -> x1, waiting for transfers between devices: none -> 20.4 us  [body(): lax.psum_scatter(jnp.einsum('tc,td->cd', gradient_in, attn, preferred_ele...]
    all_gather x0 -> x1, blocking collectives: none -> 11.1 us  [body(): lax.all_gather(field_in, lane_axis).sum(axis=0)]
    unnamed x30 -> x26, local copies, waits for them, and re-layouts: 6.73 us -> 3.18 us
  transfers between devices with their start and end apart: 2 -> 1, of which waited for: 2 -> 1; matrix products, arithmetic and copies ran while one was open for 7% -> 7% of each run, Pallas kernels for 0% -> 0%
where the time goes in v1:
time: 259 us; the launch traced here: 258 us
  local copies, waits for them, and re-layouts  75.7 us (29%)
  matrix products  51.8 us (20%)
  blocking collectives  46.1 us (18%)
  other arithmetic  40.5 us (16%)
  waiting for transfers between devices  20.4 us (8%)
  between operations  14.9 us (6%)
  loops' own time  8.39 us (3%)
    broadcast_in_dim x4, local copies, waits for them, and re-layouts, combine(): jnp.where(dilation_match[None, :, :, None], dilated_row_sum[:, None], 0.0)  23 us
    dot_general x4, matrix products, one_group(): jnp.einsum('shqk,skhd->sqhd', weights.astype(jnp.bfloat16), value_part, p...  22.5 us
    another operation x3, local copies, waits for them, and re-layouts, select_rows(): tensor.reshape(segment_height // RATE, RATE, ATTENTION_HEADS, HEAD_SIZE)  21.5 us
    reduce_scatter x1, waiting for transfers between devices, body(): lax.psum_scatter(jnp.einsum('tc,td->cd', gradient_in, attn, preferred_ele...  20.4 us
    all_gather x1, blocking collectives, body(): lax.all_gather(key_sel.reshape(picked, D), 'seq', axis=0, tiled=True)  18.4 us
    all_gather x1, blocking collectives, body(): lax.all_gather(value_sel.reshape(picked, D), 'seq', axis=0, tiled=True)  16.6 us
    reduce_sum x4, other arithmetic, one_group(): totals = jnp.sum(weights, axis=-1)  16.4 us
    dot_general x4, matrix products, one_group(): jnp.einsum('sqhd,skhd->shqk', query_part, key_part, preferred_element_typ...  13.4 us
  transfers between devices with their start and end apart: 1, of which 1 were waited for; matrix products, arithmetic and copies ran while one was open for 7% of the time, Pallas kernels for 0%

profile of v1, /device:TPU:0, one launch (start us, length us, event | category | flops | bytes accessed | tf_op | source)
XLA Modules:
  0.0 257.9 jit_solution(16686336795253595282)
XLA Ops:
  9.7 2.8 %convolution_convert_fusion.3 = bf16[1024,768]{0,1:T(8,128)(2,1)S(1)} fusion(bf16[768,768]{1,0:T(8,128)(2,1)} %param.13, bf16[1,1024,768]{2,1,0:T(8,128)(2,1)S(1)} %copy-done), kind=kOutput, calls=%fused_computation.46 | convolution fusion | flops 1208745984 | bytes 4325376 | tf_op jit(solution)/shard_map/dot_general | solution.py:16
  12.5 2.6 %convolution_convert_fusion.2 = bf16[1024,768]{0,1:T(8,128)(2,1)} fusion(bf16[768,768]{1,0:T(8,128)(2,1)S(1)} %copy-done.9, bf16[1,1024,768]{2,1,0:T(8,128)(2,1)S(1)} %copy-done), kind=kOutput, calls=%fused_computation.45 | convolution fusion | flops 1208745984 | bytes 4325376 | tf_op jit(solution)/shard_map/dot_general | solution.py:16
  15.1 2.6 %convolution_convert_fusion.1 = bf16[1024,768]{0,1:T(8,128)(2,1)} fusion(bf16[768,768]{1,0:T(8,128)(2,1)S(1)} %copy-done.10, bf16[1,1024,768]{2,1,0:T(8,128)(2,1)S(1)} %copy-done), kind=kOutput, calls=%fused_computation.44 | convolution fusion | flops 1208745984 | bytes 4325376 | tf_op jit(solution)/shard_map/dot_general | solution.py:16
  17.7 2.8 %copy.59 = bf16[1024,768]{1,0:T(8,128)(2,1)} copy(bf16[1024,768]{0,1:T(8,128)(2,1)} %convolution_convert_fusion.1) | data formatting | bytes 3145728 | tf_op jit(solution)/shard_map/convert_element_type | solution.py:16
  20.4 1.6 copy.55
  22.1 1.6 copy.57
  23.6 7.2 %reshape_reshape.22 = bf16[64,16,16,48]{3,2,1,0:T(8,128)(2,1)} reshape(bf16[1024,768]{1,0:T(8,128)(2,1)} %copy.57) | data formatting | bytes 3145728 | tf_op jit(solution)/shard_map/reshape;reshape | solution.py:21
  30.8 7.2 %reshape_reshape.21 = bf16[64,16,16,48]{3,2,1,0:T(8,128)(2,1)} reshape(bf16[1024,768]{1,0:T(8,128)(2,1)} %copy.55) | data formatting | bytes 3145728 | tf_op jit(solution)/shard_map/reshape;reshape | solution.py:21
  38.0 7.2 %reshape_reshape.23 = bf16[64,16,16,48]{3,2,1,0:T(8,128)(2,1)} reshape(bf16[1024,768]{1,0:T(8,128)(2,1)} %copy.59) | data formatting | bytes 3145728 | tf_op jit(solution)/shard_map/reshape;reshape | solution.py:21
  45.2 9.0 %multiply_reduce_fusion.1 = (bf16[16,64,48]{2,0,1:T(8,128)(2,1)S(1)}, bf16[16,64,48]{2,0,1:T(8,128)(2,1)}, bf16[16,64,48]{2,0,1:T(8,128)(2,1)}) fusion(f32[16,16]{0,1:T(8,128)S(1)} %copy.90, bf16[64,16,16,48]{3,2,1,0:T(8,128)(2,1)} %reshape_reshape.22, bf16[64,16,16,48]{3,2,1,0:T(8,128)(2,1)} %reshape_reshape.23, bf16[64,16,16,48]{3,2,1,0:T(8,128)(2,1)} %reshape_reshape.21), kind=kLoop, calls=%fused_computation.25 | loop fusion | flops 6930432 | bytes 5014528
  55.1 1.2 reshape.266
  56.3 1.2 reshape.263
  57.5 18.4 %all_gather.12 = bf16[512,768]{1,0:T(8,128)(2,1)} all-gather(bf16[64,768]{1,0:T(8,128)(2,1)S(1)} %reshape.263), channel_id=1, replica_groups=mesh['dp'=4,'seq'=8] {'seq'}, dimensions={0}, use_global_device_ids=true | all-gather | bytes 884736 | tf_op jit(solution)/shard_map/all_gather | solution.py:104
  76.0 2.3 copy.56
  78.3 16.6 %all_gather.13 = bf16[512,768]{1,0:T(8,128)(2,1)} all-gather(bf16[64,768]{1,0:T(8,128)(2,1)S(1)} %reshape.266), channel_id=1, replica_groups=mesh['dp'=4,'seq'=8] {'seq'}, dimensions={0}, use_global_device_ids=true | all-gather | bytes 884736 | tf_op jit(solution)/shard_map/all_gather | solution.py:105
  94.9 2.3 copy.60
  97.3 1.8 bitcast_reduce_fusion
  99.1 1.4 fusion.34
  101.1 1.0 copy.61
  102.1 1.7 broadcast_in_dim.151
  103.8 1.3 broadcast_in_dim.152
  105.1 1.7 broadcast_in_dim.159
  106.8 1.3 broadcast_in_dim.160
  108.2 68.3 %while.15 = (s32[]{:T(128)}, f32[4,1,4,1024]{3,2,1,0:T(4,128)}, f32[4,1,4,1024]{3,2,1,0:T(4,128)}, f32[4,1,1024,4,48]{2,4,3,1,0:T(8,128)}, s32[4]{0:T(128)S(1)},...) while((s32[]{:T(128)}, f32[4,1,4,1024]{3,2,1,0:T(4,128)}, ...), condition=%wide.region_3.4_spmd.clone, body=%wide.region_0.3_spmd.clone.sunk | while | flops 851437568 | bytes 52434116 | solution.py:56
  111.7 3.4 %fusion.70 = (f32[4,1024]{1,0:T(4,128)S(1)}, f32[4,1024,1024]{1,2,0:T(8,128)S(1)}) fusion(pred[1024]{0:T(1024)(128)(4,1)S(1)} %add_compare_fusion.4, bf16[1,1024,4,4,48]{1,4,3,2,0:T(8,128)(2,1)S(1)} %get-tuple-element.213, s32[]{:T(128)S(6)} %select_n.128, bf16[1,1024,4,4,48]{1,4,3,2,0:T(8,128)(2,1)S(1)} %get-tuple-element.212), kind=kOutput, calls=%fused_computation.3.clone.1 | convolution fusion | flops 415232000 | bytes 17582080 | tf_op jit(solution)/shard_map/while/body/eval_jaxpr/sqhd,skhd->shqk/dot_general | solution.py:41
  115.1 4.1 %fusion.71 = f32[4,1024]{1,0:T(4,128)S(1)} fusion(f32[4,1024,1024]{1,2,0:T(8,128)S(1)} %get-tuple-element.177, f32[4,1024]{1,0:T(4,128)S(1)} %get-tuple-element.178, pred[1024]{0:T(1024)(128)(4,1)S(1)} %add_compare_fusion.4), kind=kLoop, calls=%fused_computation.5.clone.1 | loop fusion | flops 16773120 | bytes 16811008 | tf_op jit(solution)/shard_map/while/body/eval_jaxpr/reduce_sum | solution.py:47
  119.2 5.7 %fusion.72 = f32[4,1,1024,4,48]{2,4,3,1,0:T(8,128)} fusion(f32[4,1,1024,4,48]{2,4,3,1,0:T(8,128)} %get-tuple-element.197, s32[]{:T(128)S(6)} %copy.99, f32[4,1024,1024]{1,2,0:T(8,128)S(1)} %get-tuple-element.177, f32[4,1024]{1,0:T(4,128)S(1)} %get-tuple-element.178, pred[1024]{0:T(1024)(128)(4,1)S(1)} %add_compare_fusion.4, ...), kind=kOutput, calls=%fused_computation.9.clone.1 | convolution fusion | flops 419430400 | bytes 17974280 | tf_op jit(solution)/shard_map/while/body/eval_jaxpr/shqk,skhd->sqhd/dot_general | solution.py:48
  128.8 3.4 %fusion.70 = (f32[4,1024]{1,0:T(4,128)S(1)}, f32[4,1024,1024]{1,2,0:T(8,128)S(1)}) fusion(pred[1024]{0:T(1024)(128)(4,1)S(1)} %add_compare_fusion.4, bf16[1,1024,4,4,48]{1,4,3,2,0:T(8,128)(2,1)S(1)} %get-tuple-element.213, s32[]{:T(128)S(6)} %select_n.128, bf16[1,1024,4,4,48]{1,4,3,2,0:T(8,128)(2,1)S(1)} %get-tuple-element.212), kind=kOutput, calls=%fused_computation.3.clone.1 | convolution fusion | flops 415232000 | bytes 17582080 | tf_op jit(solution)/shard_map/while/body/eval_jaxpr/sqhd,skhd->shqk/dot_general | solution.py:41
  132.1 4.1 %fusion.71 = f32[4,1024]{1,0:T(4,128)S(1)} fusion(f32[4,1024,1024]{1,2,0:T(8,128)S(1)} %get-tuple-element.177, f32[4,1024]{1,0:T(4,128)S(1)} %get-tuple-element.178, pred[1024]{0:T(1024)(128)(4,1)S(1)} %add_compare_fusion.4), kind=kLoop, calls=%fused_computation.5.clone.1 | loop fusion | flops 16773120 | bytes 16811008 | tf_op jit(solution)/shard_map/while/body/eval_jaxpr/reduce_sum | solution.py:47
  136.2 5.6 %fusion.72 = f32[4,1,1024,4,48]{2,4,3,1,0:T(8,128)} fusion(f32[4,1,1024,4,48]{2,4,3,1,0:T(8,128)} %get-tuple-element.197, s32[]{:T(128)S(6)} %copy.99, f32[4,1024,1024]{1,2,0:T(8,128)S(1)} %get-tuple-element.177, f32[4,1024]{1,0:T(4,128)S(1)} %get-tuple-element.178, pred[1024]{0:T(1024)(128)(4,1)S(1)} %add_compare_fusion.4, ...), kind=kOutput, calls=%fused_computation.9.clone.1 | convolution fusion | flops 419430400 | bytes 17974280 | tf_op jit(solution)/shard_map/while/body/eval_jaxpr/shqk,skhd->sqhd/dot_general | solution.py:48
  145.8 3.3 %fusion.70 = (f32[4,1024]{1,0:T(4,128)S(1)}, f32[4,1024,1024]{1,2,0:T(8,128)S(1)}) fusion(pred[1024]{0:T(1024)(128)(4,1)S(1)} %add_compare_fusion.4, bf16[1,1024,4,4,48]{1,4,3,2,0:T(8,128)(2,1)S(1)} %get-tuple-element.213, s32[]{:T(128)S(6)} %select_n.128, bf16[1,1024,4,4,48]{1,4,3,2,0:T(8,128)(2,1)S(1)} %get-tuple-element.212), kind=kOutput, calls=%fused_computation.3.clone.1 | convolution fusion | flops 415232000 | bytes 17582080 | tf_op jit(solution)/shard_map/while/body/eval_jaxpr/sqhd,skhd->shqk/dot_general | solution.py:41
  149.1 4.1 %fusion.71 = f32[4,1024]{1,0:T(4,128)S(1)} fusion(f32[4,1024,1024]{1,2,0:T(8,128)S(1)} %get-tuple-element.177, f32[4,1024]{1,0:T(4,128)S(1)} %get-tuple-element.178, pred[1024]{0:T(1024)(128)(4,1)S(1)} %add_compare_fusion.4), kind=kLoop, calls=%fused_computation.5.clone.1 | loop fusion | flops 16773120 | bytes 16811008 | tf_op jit(solution)/shard_map/while/body/eval_jaxpr/reduce_sum | solution.py:47
  153.2 5.6 %fusion.72 = f32[4,1,1024,4,48]{2,4,3,1,0:T(8,128)} fusion(f32[4,1,1024,4,48]{2,4,3,1,0:T(8,128)} %get-tuple-element.197, s32[]{:T(128)S(6)} %copy.99, f32[4,1024,1024]{1,2,0:T(8,128)S(1)} %get-tuple-element.177, f32[4,1024]{1,0:T(4,128)S(1)} %get-tuple-element.178, pred[1024]{0:T(1024)(128)(4,1)S(1)} %add_compare_fusion.4, ...), kind=kOutput, calls=%fused_computation.9.clone.1 | convolution fusion | flops 419430400 | bytes 17974280 | tf_op jit(solution)/shard_map/while/body/eval_jaxpr/shqk,skhd->sqhd/dot_general | solution.py:48
  162.8 3.3 %fusion.70 = (f32[4,1024]{1,0:T(4,128)S(1)}, f32[4,1024,1024]{1,2,0:T(8,128)S(1)}) fusion(pred[1024]{0:T(1024)(128)(4,1)S(1)} %add_compare_fusion.4, bf16[1,1024,4,4,48]{1,4,3,2,0:T(8,128)(2,1)S(1)} %get-tuple-element.213, s32[]{:T(128)S(6)} %select_n.128, bf16[1,1024,4,4,48]{1,4,3,2,0:T(8,128)(2,1)S(1)} %get-tuple-element.212), kind=kOutput, calls=%fused_computation.3.clone.1 | convolution fusion | flops 415232000 | bytes 17582080 | tf_op jit(solution)/shard_map/while/body/eval_jaxpr/sqhd,skhd->shqk/dot_general | solution.py:41
  166.1 4.1 %fusion.71 = f32[4,1024]{1,0:T(4,128)S(1)} fusion(f32[4,1024,1024]{1,2,0:T(8,128)S(1)} %get-tuple-element.177, f32[4,1024]{1,0:T(4,128)S(1)} %get-tuple-element.178, pred[1024]{0:T(1024)(128)(4,1)S(1)} %add_compare_fusion.4), kind=kLoop, calls=%fused_computation.5.clone.1 | loop fusion | flops 16773120 | bytes 16811008 | tf_op jit(solution)/shard_map/while/body/eval_jaxpr/reduce_sum | solution.py:47
  170.2 5.6 %fusion.72 = f32[4,1,1024,4,48]{2,4,3,1,0:T(8,128)} fusion(f32[4,1,1024,4,48]{2,4,3,1,0:T(8,128)} %get-tuple-element.197, s32[]{:T(128)S(6)} %copy.99, f32[4,1024,1024]{1,2,0:T(8,128)S(1)} %get-tuple-element.177, f32[4,1024]{1,0:T(4,128)S(1)} %get-tuple-element.178, pred[1024]{0:T(1024)(128)(4,1)S(1)} %add_compare_fusion.4, ...), kind=kOutput, calls=%fused_computation.9.clone.1 | convolution fusion | flops 419430400 | bytes 17974280 | tf_op jit(solution)/shard_map/while/body/eval_jaxpr/shqk,skhd->sqhd/dot_general | solution.py:48
  178.2 4.9 %broadcast_in_dim.156 = f32[64,16,16,48]{3,2,1,0:T(8,128)} broadcast(f32[64,16,48]{2,1,0:T(8,128)} %copy.61), dimensions={0,2,3} | broadcast | bytes 3342336 | tf_op jit(solution)/shard_map/jit(_where)/broadcast_in_dim | solution.py:74
  183.1 6.5 %copy.63 = f32[1024,16,48]{0,2,1:T(8,128)} copy(f32[1024,16,48]{2,1,0:T(8,128)} %bitcast.162) | data formatting | bytes 6291456 | tf_op jit(solution)/shard_map/jit(_where)/broadcast_in_dim | solution.py:74
  189.7 4.0 %fusion.32 = bf16[1024,16,48]{0,2,1:T(8,128)(2,1)S(1)} fusion(f32[1024,16,48]{0,2,1:T(8,128)} %copy.63, f32[4,1,1024,4,48]{2,4,3,1,0:T(8,128)} %get-tuple-element.52, f32[1024,16]{0,1:T(8,128)S(1)} %get-tuple-element.101, f32[1024,16]{0,1:T(8,128)S(1)} %get-tuple-element.103, f32[1024,16]{0,1:T(8,128)S(1)} %get-tuple-element.102, ...), kind=kLoop, calls=%fused_computation.37 | loop fusion | flops 5505024 | bytes 8078336 | tf_op jit(solution)/shard_map/convert_element_type | solution.py:84
  193.8 2.9 %convolution_bitcast_fusion = f32[768,768]{0,1:T(8,128)} fusion(bf16[1024,768]{0,1:T(8,128)(2,1)S(1)} %bitcast.168, bf16[1,1024,768]{2,1,0:T(8,128)(2,1)S(1)} %copy-done.8), kind=kOutput, calls=%fused_computation.42 | convolution fusion | flops 1207959552 | bytes 5505024 | tf_op jit(solution)/shard_map/tc,td->cd/dot_general | solution.py:128
  196.6 3.0 %copy.88 = f32[768,768]{1,0:T(8,128)} copy(f32[768,768]{0,1:T(8,128)} %convolution_bitcast_fusion) | data formatting | bytes 4718592
  199.7 7.9 %broadcast_in_dim.157 = f32[1024,768]{1,0:T(8,128)} reshape(f32[64,16,16,48]{3,2,1,0:T(8,128)} %broadcast_in_dim.156) | data formatting | bytes 6291456 | tf_op jit(solution)/shard_map/jit(_where)/broadcast_in_dim | solution.py:74
  207.6 3.5 %copy.62 = f32[1024,768]{0,1:T(8,128)} copy(f32[1024,768]{1,0:T(8,128)} %broadcast_in_dim.157) | data formatting | bytes 6291456 | tf_op jit(solution)/shard_map/jit(_where)/broadcast_in_dim | solution.py:74
  211.2 3.9 %fusion.31 = bf16[1024,768]{0,1:T(8,128)(2,1)S(1)} fusion(f32[1024,768]{0,1:T(8,128)} %copy.62, f32[4,1,1024,4,48]{2,4,3,1,0:T(8,128)} %get-tuple-element.52, f32[1024,16]{0,1:T(8,128)S(1)} %get-tuple-element.101, f32[1024,16]{0,1:T(8,128)S(1)} %get-tuple-element.103, f32[1024,16]{0,1:T(8,128)S(1)} %get-tuple-element.102, ...), kind=kLoop, calls=%fused_computation.36 | loop fusion | flops 5505024 | bytes 8078336 | tf_op jit(solution)/shard_map/convert_element_type | solution.py:84
  215.2 2.6 %fusion.40 = bf16[1,1024,768]{2,1,0:T(8,128)(2,1)} fusion(bf16[1024,768]{0,1:T(8,128)(2,1)S(1)} %fusion.31, bf16[768,768]{1,0:T(8,128)(2,1)S(1)} %copy-done.11), kind=kOutput, calls=%fused_computation.53 | convolution fusion | flops 1208745984 | bytes 4325376 | tf_op jit(solution)/shard_map/dot_general | solution.py:125
  217.8 20.4 %reduce-scatter.4.cloned.1.call-done = f32[96,768]{1,0:T(8,128)} async-done(((f32[768,768]{1,0:T(8,128)}), f32[96,768]{1,0:T(8,128)}) %reduce-scatter.4.cloned.1.call-update) | async-done | bytes 294928 | tf_op jit(solution)/shard_map/reduce_scatter | solution.py:127
  238.2 1.0 convert_element_type.80
  239.1 11.1 %all-gather = bf16[384,768]{1,0:T(8,128)(2,1)S(1)} all-gather(bf16[96,768]{1,0:T(8,128)(2,1)S(1)} %convert_element_type.80), channel_id=2, replica_groups=mesh['dp'=4,'seq'=8] {'dp'}, dimensions={0}, use_global_device_ids=true | all-gather | bytes 737280 | tf_op jit(solution)/shard_map/all_gather | solution.py:133
  (57 shorter events, 13.8 us)
Async XLA Ops:
  7.2 2.5 copy-start
  7.2 231.0 %reduce-scatter.4.cloned.1.call-start = ((), (), s32[]{:S(2)}) async-start(), calls=%async_computation.1 | async-start | bytes 2654208 | tf_op jit(solution)/shard_map/reduce_scatter | solution.py:127
  9.6 2.8 %copy-start.9 = (bf16[768,768]{1,0:T(8,128)(2,1)S(1)}, bf16[768,768]{1,0:T(8,128)(2,1)}, u32[]{:S(2)}) copy-start(bf16[768,768]{1,0:T(8,128)(2,1)} %param.14) | copy-start | bytes 3538948
  12.5 2.6 %copy-start.10 = (bf16[768,768]{1,0:T(8,128)(2,1)S(1)}, bf16[768,768]{1,0:T(8,128)(2,1)}, u32[]{:S(2)}) copy-start(bf16[768,768]{1,0:T(8,128)(2,1)} %param.15) | copy-start | bytes 3538948
  17.7 2.8 %copy-start.2 = (bf16[1024,768]{0,1:T(8,128)(2,1)S(1)}, bf16[1024,768]{0,1:T(8,128)(2,1)}, u32[]{:S(2)}) copy-start(bf16[1024,768]{0,1:T(8,128)(2,1)} %convolution_convert_fusion.2) | copy-start | bytes 4718596
  57.5 39.7 %copy-start.3 = (bf16[16,64,48]{1,2,0:T(8,128)(2,1)S(1)}, bf16[16,64,48]{1,2,0:T(8,128)(2,1)}, u32[]{:S(2)}) copy-start(bf16[16,64,48]{1,2,0:T(8,128)(2,1)} %copy.80) | copy-start | bytes 294916
  76.0 21.2 %copy-start.6 = (s32[512]{0:T(512)S(1)}, s32[512]{0:T(512)}, u32[]{:S(2)}) copy-start(s32[512]{0:T(512)} %iota_multiply_fusion) | copy-start | bytes 6148
  76.0 21.2 %copy-start.7 = (s32[16]{0:T(128)S(1)}, s32[16]{0:T(128)}, u32[]{:S(2)}) copy-start(s32[16]{0:T(128)} %param.12) | copy-start | bytes 196
  97.2 3.2 %copy-start.4 = (bf16[512,768]{0,1:T(8,128)(2,1)S(1)}, bf16[512,768]{0,1:T(8,128)(2,1)}, u32[]{:S(2)}) copy-start(bf16[512,768]{0,1:T(8,128)(2,1)} %copy.60) | copy-start | bytes 2359300
  99.1 1.4 copy-start.5
  189.7 4.0 %copy-start.8 = (bf16[1,1024,768]{2,1,0:T(8,128)(2,1)S(1)}, bf16[1,1024,768]{2,1,0:T(8,128)(2,1)}, u32[]{:S(2)}) copy-start(bf16[1,1024,768]{2,1,0:T(8,128)(2,1)} %param.17) | copy-start | bytes 4718596
  211.2 4.0 %copy-start.11 = (bf16[768,768]{1,0:T(8,128)(2,1)S(1)}, bf16[768,768]{1,0:T(8,128)(2,1)}, u32[]{:S(2)}) copy-start(bf16[768,768]{1,0:T(8,128)(2,1)} %param.16) | copy-start | bytes 3538948
  215.1 35.9 %copy-start.1 = (bf16[1,1024,768]{2,1,0:T(8,128)(2,1)S(1)}, bf16[1,1024,768]{2,1,0:T(8,128)(2,1)}, u32[]{:S(2)}) copy-start(bf16[1,1024,768]{2,1,0:T(8,128)(2,1)} %param.10) | copy-start | bytes 4718596
Sparse Core Ops, SparseCore 0:
  199.8 38.3 reduce-scatter.3
